TPU v7x, 32 devices: a whole 2x2x4 slice. The times are simulated.
32 devices in a mesh: group: 2 (over x), dom: 16 (over z, y, core).
Axes of the slice: x: 2, y: 2, z: 4, core: 2. Of those that a mesh axis runs over, the one named last changes fastest.
Arguments:
- features: bfloat16 [8192, 512], P(('group', 'dom')), may hold values from -6 to 6
- tile_columns: int32 [32, 2, 4], P(('group', 'dom')), may hold values from 0 to 1
- tile_values: bfloat16 [32, 2, 4, 128, 128], P(('group', 'dom')), as said below
- send_rows: int32 [32, 16, 16], P(('group', 'dom')), may hold values from 0 to 255
- send_count: int32 [32, 16], P(('group', 'dom')), may hold values from 0 to 16, as said below
- ghost_target: int32 [32, 16, 16], P(('group', 'dom')), may hold values from 0 to 255
- query_rows: int32 [32, 512], P(('group', 'dom')), may hold values from 0 to 255
- positive_cand: int32 [32, 512], P(('group', 'dom')), may hold values from 0 to 63
- negative_rows: int32 [32, 32], P(('group', 'dom')), may hold values from 0 to 255
- weight_self: bfloat16 [512, 512], replicated, may hold values from -0.25 to 0.25
- weight_neigh: bfloat16 [512, 512], replicated, may hold values from -0.75 to 0.75
Outputs:
- embeddings: bfloat16 [8192, 512], P(('group', 'dom'))
- weight_grads: bfloat16 [1024, 512], P('dom')
Inputs may be any that keep to these rules, and one draw needn't show every extreme that they name: `send_count`: no device sends rows to its own index of dom; in every group one index of dom receives exactly 16 rows from every other index. `tile_values`: weights are zero or between 0.5 and 1.
All inputs are finite; a program needn't handle non-finite values.
Results may differ from a plain program's by a relative error of at most 0.015.
Values may be sent and summed in bfloat16 or wider, within the bound.
No kernel may reach another device: no remote copies, remote signals or barrier semaphores. Data moves between devices by JAX's collectives and lax.ppermute only.
A program may use at most 64 MiB of HBM per device.

v0:
```python
import math
import jax
import jax.numpy as jnp
from jax import lax
from jax.sharding import PartitionSpec as P

LOSS_FACTOR = 64.0
EPSILON = 1e-05


def score_grads(scores, positive, cand_total, query_total):
    sigma = jax.nn.sigmoid(scores)
    dscore = jnp.where(positive, sigma - 1.0, sigma / (cand_total - 1.0)) * (
        LOSS_FACTOR / query_total
    )
    return dscore.astype(jnp.bfloat16)


def transpose_dot(left, right):
    return lax.dot_general(
        left, right, (((0,), (0,)), ((), ())), preferred_element_type=jnp.float32
    )


def on_device(
    features,
    tile_columns,
    tile_values,
    send_rows,
    send_count,
    ghost_target,
    query_rows,
    positive_cand,
    negative_rows,
    weight_self,
    weight_neigh,
):
    node_count, width = features.shape
    row_blocks, tiles_row, tile_size = (
        tile_values.shape[1],
        tile_values.shape[2],
        tile_values.shape[3],
    )
    slot_count = send_rows.shape[2]
    group_count = lax.axis_size("group")
    score_factor = 1.0 / math.sqrt(width)
    outgoing = features[send_rows[0]]
    flags = (jnp.arange(slot_count, dtype=jnp.int32)[None, :] < send_count[0][:, None]).astype(
        jnp.bfloat16
    )
    received, flags_in = (
        lax.all_to_all(outgoing, "dom", split_axis=0, concat_axis=0, tiled=True),
        lax.all_to_all(flags, "dom", split_axis=0, concat_axis=0, tiled=True),
    )
    blocks = features.reshape(row_blocks, tile_size, width)
    picked = blocks[tile_columns[0]]
    local = jnp.einsum(
        "rtij,rtjd->rid", tile_values[0], picked, preferred_element_type=jnp.float32
    ).reshape(node_count, width)
    row_weight = jnp.sum(tile_values[0].astype(jnp.float32), axis=(1, 3)).reshape(node_count)
    live = flags_in.astype(jnp.float32)
    targets = ghost_target[0].reshape(-1)
    weighted = (received.astype(jnp.float32) * live[:, :, None]).reshape(-1, width)
    ghost_sum = jnp.zeros((node_count, width), jnp.float32).at[targets].add(weighted)
    ghost_count = jnp.zeros((node_count,), jnp.float32).at[targets].add(live.reshape(-1))
    degree = 1.0 + row_weight + ghost_count
    aggregate = ((local + ghost_sum) / degree[:, None]).astype(jnp.bfloat16)
    pre = jnp.dot(features, weight_self, preferred_element_type=jnp.float32) + jnp.dot(
        aggregate, weight_neigh, preferred_element_type=jnp.float32
    )
    scale = lax.rsqrt(jnp.mean(pre * pre, axis=-1, keepdims=True) + EPSILON)
    embeds = (pre * scale).astype(jnp.bfloat16)
    queries = embeds[query_rows[0]]
    own_negs = embeds[negative_rows[0]]
    neg_count = own_negs.shape[0]
    query_total = queries.shape[0]
    cand_total = neg_count * group_count
    targets_pos = positive_cand[0][:, None]
    all_negs = lax.all_gather(own_negs, "group", axis=0, tiled=True)
    scores = score_factor * jnp.dot(queries, all_negs.T, preferred_element_type=jnp.float32)
    positive = targets_pos == jnp.arange(cand_total, dtype=jnp.int32)[None, :]
    dscore = score_grads(scores, positive, cand_total, query_total)
    query_grad = score_factor * jnp.dot(dscore, all_negs, preferred_element_type=jnp.float32)
    neg_grad = lax.psum_scatter(
        (score_factor * transpose_dot(dscore, queries)).astype(jnp.bfloat16),
        "group",
        scatter_dimension=0,
        tiled=True,
    ).astype(jnp.float32)
    emb_grad = jnp.zeros((node_count, width), jnp.float32)
    emb_grad = emb_grad.at[query_rows[0]].add(query_grad)
    emb_grad = emb_grad.at[negative_rows[0]].add(neg_grad)
    inner = jnp.mean(pre * emb_grad, axis=-1, keepdims=True)
    pre_grad = (scale * emb_grad - pre * scale * scale * scale * inner).astype(jnp.bfloat16)
    stacked = jnp.concatenate([features, aggregate], axis=1)
    shard = lax.psum_scatter(
        transpose_dot(stacked, pre_grad), "dom", scatter_dimension=0, tiled=True
    )
    summed = lax.psum(shard.astype(jnp.bfloat16), "group")
    return (embeds, summed)


def solution(mesh):
    placed = (
        P(("group", "dom"), None),
        P(("group", "dom"), None, None),
        P(("group", "dom"), None, None, None, None),
        P(("group", "dom"), None, None),
        P(("group", "dom"), None),
        P(("group", "dom"), None, None),
        P(("group", "dom"), None),
        P(("group", "dom"), None),
        P(("group", "dom"), None),
        P(),
        P(),
    )
    return jax.shard_map(
        on_device,
        mesh=mesh,
        in_specs=placed,
        out_specs=(P(("group", "dom"), None), P("dom", None)),
        check_vma=False,
    )
```

profile of v0, /device:TPU:0, one launch (start us, length us, event | category | flops | bytes accessed | tf_op | source)
XLA Modules:
  0.0 157.0 jit_solution(12821754926774188139)
XLA Ops:
  7.2 1.4 compare_convert_fusion
  8.6 7.4 %all-to-all-start.1 = ((bf16[16,1,16]{2,1,0:T(2,128)(2,1)}), bf16[16,1,16]{2,1,0:T(2,128)(2,1)S(1)}, u32[]{:S(2)}, u32[]{:S(2)}) async-start(bf16[16,1,16]{2,1,0:T(2,128)(2,1)} %compare_convert_fusion), calls=%async_computation.1 | async-start | bytes 16384 | tf_op jit(solution)/shard_map/all_to_all | solution.py:53
  16.0 0.7 fusion.17
  16.7 0.7 compare_select_fusion.3
  17.4 0.8 reshape_squeeze.3
  18.2 1.1 convert_reduce_fusion
  19.3 0.7 compare_select_fusion.1
  20.0 0.7 compare_select_fusion
  20.8 1.4 fusion.19
  22.3 1.9 %gather_fusion.1 = bf16[256,512]{1,0:T(8,128)(2,1)} fusion(bf16[256,512]{1,0:T(8,128)(2,1)S(1)} %copy-done.2, s32[1024]{0:T(1024)S(1)} %pad_clamp_fusion.2), kind=kCustom, calls=%fused_computation.1 | custom fusion | bytes 525312 | tf_op jit(solution)/shard_map/gather | solution.py:47
  24.1 0.6 gather_fusion
  24.8 6.0 %all-to-all-start = ((bf16[16,16,512]{2,1,0:T(8,128)(2,1)}), bf16[16,16,512]{2,1,0:T(8,128)(2,1)S(1)}, u32[]{:S(2)}, u32[]{:S(2)}) async-start(bf16[16,16,512]{2,1,0:T(8,128)(2,1)} %bitcast.10), calls=%async_computation | async-start | bytes 524288 | tf_op jit(solution)/shard_map/all_to_all | solution.py:52
  30.9 0.3 fusion.9
  31.3 2.3 %scatter_fusion.1 = f32[256]{0:T(256)S(1)} fusion(f32[256]{0:T(256)S(1)} %add_bitcast_fusion, s32[256]{0:T(256)S(1)} %bitcast.51, f32[256]{0:T(256)S(1)} %reshape.273), kind=kCustom, calls=%fused_computation.5 | custom fusion | flops 256 | bytes 4096 | tf_op jit(solution)/shard_map/scatter-add | solution.py:65
  33.6 7.2 %all-to-all-done = bf16[16,16,512]{2,1,0:T(8,128)(2,1)S(1)} async-done(((bf16[16,16,512]{2,1,0:T(8,128)(2,1)}), bf16[16,16,512]{2,1,0:T(8,128)(2,1)S(1)}, u32[]{:S(2)}, u32[]{:S(2)}) %all-to-all-start) | async-done | bytes 262176 | tf_op jit(solution)/shard_map/all_to_all | solution.py:52
  40.9 2.3 %scatter_fusion = f32[256,512]{1,0:T(8,128)S(1)} fusion(f32[256,512]{1,0:T(8,128)S(1)} %bitcast.46, s32[256]{0:T(256)S(1)} %bitcast.52, f32[256,512]{1,0:T(8,128)S(1)} %bitcast.49), kind=kCustom, calls=%fused_computation.4 | custom fusion | flops 131072 | bytes 1573888 | tf_op jit(solution)/shard_map/scatter-add | solution.py:64
  43.3 0.4 multiply_reduce_fusion.1
  43.9 0.6 gather_fusion.3
  44.5 4.6 %all-gather = bf16[64,512]{1,0:T(8,128)(2,1)S(1)} all-gather(bf16[32,512]{1,0:T(8,128)(2,1)S(1)} %gather_fusion.3), channel_id=2, replica_groups=mesh['group'=2,'dom'=16] {'group'}, dimensions={0}, use_global_device_ids=true | all-gather | bytes 98304 | tf_op jit(solution)/shard_map/all_gather | solution.py:79
  49.1 2.0 %gather_fusion.2 = bf16[512,512]{1,0:T(8,128)(2,1)S(1)} fusion(bf16[256,512]{1,0:T(8,128)(2,1)S(1)} %multiply_convert_fusion, s32[1024]{0:T(1024)S(1)} %pad_clamp_fusion.1), kind=kCustom, calls=%fused_computation.2 | custom fusion | bytes 1050624 | tf_op jit(solution)/shard_map/gather | solution.py:73
  51.1 0.3 multiply_convert_fusion.1
  51.4 0.8 fusion.4
  52.3 0.3 convolution_multiply_fusion
  52.6 3.7 %scatter_custom_fusion.2 = f32[256,512]{1,0:T(8,128)S(1)} fusion(s32[512]{0:T(512)S(1)} %bitcast.54, f32[512,512]{1,0:T(8,128)S(1)} %convolution_multiply_fusion, f32[]{:T(128)} %constant.14.clone.1), kind=kCustom, calls=%fused_computation.31 | custom fusion | flops 262144 | bytes 524292 | tf_op jit(solution)/shard_map/scatter-add | solution.py:91
  56.4 4.3 %reduce-scatter.3.cloned.1.call-done = bf16[32,512]{1,0:T(8,128)(2,1)} async-done(((bf16[64,512]{1,0:T(8,128)(2,1)}), bf16[32,512]{1,0:T(8,128)(2,1)}) %reduce-scatter.3.cloned.1.call-update) | async-done | bytes 32784 | tf_op jit(solution)/shard_map/reduce_scatter | solution.py:84
  60.6 1.2 scatter_custom_fusion.3
  61.9 0.1 multiply_reduce_fusion
  62.0 2.0 %fusion.5 = f32[1024,512]{1,0:T(8,128)} fusion(bf16[256,512]{1,0:T(8,128)(2,1)S(1)} %divide_convert_fusion, bf16[256,512]{1,0:T(8,128)(2,1)S(1)} %copy-done.2, f32[256,512]{1,0:T(8,128)S(1)} %scatter_custom_fusion.3, f32[256,512]{1,0:T(8,128)S(1)} %get-tuple-element.3, f32[256]{0:T(256)S(1)} %broadcast_multiply_fusion, f32[256]{0:T(256)S(1)} %add_rsqrt_fusion), kind=kOutput, calls=%fused_computation.17 | convolution fusion | flops 270401536 | bytes 3672064 | tf_op jit(solution)/shard_map/dot_general | solution.py:20
  64.0 62.2 %reduce-scatter.5.cloned.1.call-done = f32[64,512]{1,0:T(8,128)} async-done(((f32[1024,512]{1,0:T(8,128)}), f32[64,512]{1,0:T(8,128)}) %reduce-scatter.5.cloned.1.call-update) | async-done | bytes 131088 | tf_op jit(solution)/shard_map/reduce_scatter | solution.py:96
  126.2 1.5 convert_element_type.66
  127.8 21.2 %all-reduce.2.cloned.1.call-done = bf16[64,512]{1,0:T(8,128)(2,1)} async-done(((bf16[64,512]{1,0:T(8,128)(2,1)}), bf16[64,512]{1,0:T(8,128)(2,1)}) %all-reduce.2.cloned.1.call-update) | async-done | bytes 65552 | tf_op jit(solution)/shard_map/psum | solution.py:99
  149.0 1.5 copy.18
  (33 shorter events, 0.9 us)
Async XLA Ops:
  7.2 36.2 %copy-start = (bf16[512,512]{1,0:T(8,128)(2,1)S(1)}, bf16[512,512]{1,0:T(8,128)(2,1)}, u32[]{:S(2)}) copy-start(bf16[512,512]{1,0:T(8,128)(2,1)} %param.21) | copy-start | bytes 1572868
  7.2 15.1 %copy-start.2 = (bf16[256,512]{1,0:T(8,128)(2,1)S(1)}, bf16[256,512]{1,0:T(8,128)(2,1)}, u32[]{:S(2)}) copy-start(bf16[256,512]{1,0:T(8,128)(2,1)} %param.11) | copy-start | bytes 786436
  8.6 16.1 %all-to-all-start.1 = ((bf16[16,1,16]{2,1,0:T(2,128)(2,1)}), bf16[16,1,16]{2,1,0:T(2,128)(2,1)S(1)}, u32[]{:S(2)}, u32[]{:S(2)}) async-start(bf16[16,1,16]{2,1,0:T(2,128)(2,1)} %compare_convert_fusion), calls=%async_computation.1 | async-start | bytes 16384 | tf_op jit(solution)/shard_map/all_to_all | solution.py:53
  22.3 8.6 %copy-start.3 = (bf16[1,2,4,128,128]{4,3,2,1,0:T(8,128)(2,1)S(1)}, bf16[1,2,4,128,128]{4,3,2,1,0:T(8,128)(2,1)}, u32[]{:S(2)}) copy-start(bf16[1,2,4,128,128]{4,3,2,1,0:T(8,128)(2,1)} %param.13) | copy-start | bytes 786436
  24.8 16.0 %all-to-all-start = ((bf16[16,16,512]{2,1,0:T(8,128)(2,1)}), bf16[16,16,512]{2,1,0:T(8,128)(2,1)S(1)}, u32[]{:S(2)}, u32[]{:S(2)}) async-start(bf16[16,16,512]{2,1,0:T(8,128)(2,1)} %bitcast.10), calls=%async_computation | async-start | bytes 524288 | tf_op jit(solution)/shard_map/all_to_all | solution.py:52
  30.8 29.9 %reduce-scatter.3.cloned.1.call-start = ((), (), s32[]{:S(2)}) async-start(), calls=%async_computation.4 | async-start | bytes 98304 | tf_op jit(solution)/shard_map/reduce_scatter | solution.py:84
  43.9 7.2 %copy-start.1 = (bf16[256,512]{1,0:T(8,128)(2,1)}, bf16[256,512]{1,0:T(8,128)(2,1)S(1)}, u32[]{:S(2)}) copy-start(bf16[256,512]{1,0:T(8,128)(2,1)S(1)} %multiply_convert_fusion) | copy-start | bytes 786436
  49.1 2.0 %copy-start.4 = (s32[1,512]{1,0:T(1,128)S(1)}, s32[1,512]{1,0:T(1,128)}, u32[]{:S(2)}) copy-start(s32[1,512]{1,0:T(1,128)} %param.18) | copy-start | bytes 6148
  52.3 74.0 %reduce-scatter.5.cloned.1.call-start = ((), (), s32[]{:S(2)}) async-start(), calls=%async_computation.5 | async-start | bytes 2228224 | tf_op jit(solution)/shard_map/reduce_scatter | solution.py:96
  64.0 85.0 %all-reduce.2.cloned.1.call-start = ((), (), s32[]{:S(2)}) async-start(), calls=%async_computation.6 | async-start | bytes 131072 | tf_op jit(solution)/shard_map/psum | solution.py:99
Sparse Core Ops, SparseCore 0:
  52.4 8.1 reduce-scatter.2
  64.4 61.8 reduce-scatter.4
  129.1 19.8 all-reduce.1
where the time goes:
time: 158 us; the launch traced here: 157 us
  waiting for transfers between devices  94.9 us (60%)
  other arithmetic  16.8 us (11%)
  between operations  14 us (9%)
  starting transfers between devices  13.6 us (9%)
  local copies, waits for them, and re-layouts  7.58 us (5%)
  matrix products  5.54 us (4%)
  blocking collectives  4.58 us (3%)
    reduce_scatter x1, waiting for transfers between devices, on_device(): lax.psum_scatter(transpose_dot(stacked, pre_grad), 'dom', scatter_dimensi...  62.2 us
    psum x1, waiting for transfers between devices, on_device(): summed = lax.psum(shard.astype(jnp.bfloat16), 'group')  21.2 us
    all_to_all x1, starting transfers between devices, on_device(): lax.all_to_all(flags, 'dom', split_axis=0, concat_axis=0, tiled=True)  7.41 us
    all_to_all x1, waiting for transfers between devices, on_device(): lax.all_to_all(outgoing, 'dom', split_axis=0, concat_axis=0, tiled=True)  7.18 us
    all_to_all x1, starting transfers between devices, on_device(): lax.all_to_all(outgoing, 'dom', split_axis=0, concat_axis=0, tiled=True)  6.02 us
    all_gather x1, blocking collectives, on_device(): all_negs = lax.all_gather(own_negs, 'group', axis=0, tiled=True)  4.58 us
    reduce_scatter x1, waiting for transfers between devices, on_device(): lax.psum_scatter((score_factor * transpose_dot(dscore, queries)).astype(j...  4.28 us
    scatter-add x1, other arithmetic, on_device(): emb_grad = emb_grad.at[query_rows[0]].add(query_grad)  3.71 us
  transfers between devices with their start and end apart: 5, of which 4 were waited for; matrix products, arithmetic and copies ran while one was open for 10% of the time, Pallas kernels for 0%

commit v1 on v0

--- a/solution.py
+++ b/solution.py
@@ -96,7 +96,10 @@
     shard = lax.psum_scatter(
         transpose_dot(stacked, pre_grad), "dom", scatter_dimension=0, tiled=True
     )
-    summed = lax.psum(shard.astype(jnp.bfloat16), "group")
+    guide_quotas = lambda w_in, device_axis: jnp.sum(
+        lax.all_gather(w_in, axis_name=device_axis), axis=0
+    )
+    summed = guide_quotas(shard.astype(jnp.bfloat16), "group")
     return (embeds, summed)
 
 

time: 158 us -> 140 us (0.89)
  waiting for transfers between devices: 94.9 us -> 73.7 us
  blocking collectives: 4.58 us -> 9.52 us
    psum x1 -> x0, waiting for transfers between devices: 21.2 us -> none  [on_device(): summed = lax.psum(shard.astype(jnp.bfloat16), 'group')]
    all_gather x0 -> x1, blocking collectives: none -> 4.93 us  [on_device(): lax.all_gather(w_in, axis_name=device_axis)]
  transfers between devices with their start and end apart: 5 -> 4, of which waited for: 4 -> 3; matrix products, arithmetic and copies ran while one was open for 10% -> 11% of each run, Pallas kernels for 0% -> 0%
where the time goes in v1:
time: 140 us
  waiting for transfers between devices  73.7 us (53%)
  other arithmetic  16.9 us (12%)
  between operations  14.3 us (10%)
  starting transfers between devices  13.5 us (10%)
  blocking collectives  9.52 us (7%)
  local copies, waits for them, and re-layouts  6.11 us (4%)
  matrix products  5.54 us (4%)
    reduce_scatter x1, waiting for transfers between devices, on_device(): lax.psum_scatter(transpose_dot(stacked, pre_grad), 'dom', scatter_dimensi...  62.2 us
    all_to_all x1, starting transfers between devices, on_device(): lax.all_to_all(flags, 'dom', split_axis=0, concat_axis=0, tiled=True)  7.41 us
    all_to_all x1, waiting for transfers between devices, on_device(): lax.all_to_all(outgoing, 'dom', split_axis=0, concat_axis=0, tiled=True)  7.18 us
    all_to_all x1, starting transfers between devices, on_device(): lax.all_to_all(outgoing, 'dom', split_axis=0, concat_axis=0, tiled=True)  6.02 us
    all_gather x1, blocking collectives, on_device(): lax.all_gather(w_in, axis_name=device_axis)  4.93 us
    all_gather x1, blocking collectives, on_device(): all_negs = lax.all_gather(own_negs, 'group', axis=0, tiled=True)  4.58 us
    reduce_scatter x1, waiting for transfers between devices, on_device(): lax.psum_scatter((score_factor * transpose_dot(dscore, queries)).astype(j...  4.28 us
    scatter-add x1, other arithmetic, on_device(): emb_grad = emb_grad.at[query_rows[0]].add(query_grad)  3.71 us
  transfers between devices with their start and end apart: 4, of which 3 were waited for; matrix products, arithmetic and copies ran while one was open for 11% of the time, Pallas kernels for 0%

profile of v1, /device:TPU:0, one launch (start us, length us, event | category | flops | bytes accessed | tf_op | source)
XLA Modules:
  0.0 139.6 jit_solution(10528709249543655062)
XLA Ops:
  7.2 1.4 %compare_convert_fusion = bf16[16,1,16]{2,1,0:T(2,128)(2,1)} fusion(s32[16]{0:T(128)} %bitcast.57), kind=kLoop, calls=%fused_computation.38 | loop fusion | flops 512 | bytes 576 | tf_op jit(solution)/shard_map/convert_element_type | solution.py:48
  8.6 7.4 %all-to-all-start.1 = ((bf16[16,1,16]{2,1,0:T(2,128)(2,1)}), bf16[16,1,16]{2,1,0:T(2,128)(2,1)S(1)}, u32[]{:S(2)}, u32[]{:S(2)}) async-start(bf16[16,1,16]{2,1,0:T(2,128)(2,1)} %compare_convert_fusion), calls=%async_computation.1 | async-start | bytes 16384 | tf_op jit(solution)/shard_map/all_to_all | solution.py:53
  16.0 0.7 fusion.17
  16.7 0.7 compare_select_fusion.3
  17.4 0.8 reshape_squeeze.3
  18.2 1.1 convert_reduce_fusion
  19.3 0.7 compare_select_fusion.1
  20.0 0.7 compare_select_fusion
  20.8 1.4 %fusion.19 = f32[256,512]{1,0:T(8,128)S(1)} fusion(bf16[256,512]{1,0:T(8,128)(2,1)} %param.11, bf16[512,512]{1,0:T(8,128)(2,1)} %param.20), kind=kOutput, calls=%fused_computation.54 | convolution fusion | flops 134217728 | bytes 1310720 | tf_op jit(solution)/shard_map/dot_general | solution.py:68
  22.3 1.9 %gather_fusion.1 = bf16[256,512]{1,0:T(8,128)(2,1)} fusion(bf16[256,512]{1,0:T(8,128)(2,1)S(1)} %copy-done.2, s32[1024]{0:T(1024)S(1)} %pad_clamp_fusion.2), kind=kCustom, calls=%fused_computation.1 | custom fusion | bytes 525312 | tf_op jit(solution)/shard_map/gather | solution.py:47
  24.1 0.6 gather_fusion
  24.8 6.0 %all-to-all-start = ((bf16[16,16,512]{2,1,0:T(8,128)(2,1)}), bf16[16,16,512]{2,1,0:T(8,128)(2,1)S(1)}, u32[]{:S(2)}, u32[]{:S(2)}) async-start(bf16[16,16,512]{2,1,0:T(8,128)(2,1)} %bitcast.10), calls=%async_computation | async-start | bytes 524288 | tf_op jit(solution)/shard_map/all_to_all | solution.py:52
  30.9 0.3 fusion.9
  31.3 2.3 %scatter_fusion.1 = f32[256]{0:T(256)S(1)} fusion(f32[256]{0:T(256)S(1)} %add_bitcast_fusion, s32[256]{0:T(256)S(1)} %bitcast.53, f32[256]{0:T(256)S(1)} %reshape.273), kind=kCustom, calls=%fused_computation.5 | custom fusion | flops 256 | bytes 4096 | tf_op jit(solution)/shard_map/scatter-add | solution.py:65
  33.6 7.2 %all-to-all-done = bf16[16,16,512]{2,1,0:T(8,128)(2,1)S(1)} async-done(((bf16[16,16,512]{2,1,0:T(8,128)(2,1)}), bf16[16,16,512]{2,1,0:T(8,128)(2,1)S(1)}, u32[]{:S(2)}, u32[]{:S(2)}) %all-to-all-start) | async-done | bytes 262176 | tf_op jit(solution)/shard_map/all_to_all | solution.py:52
  40.9 2.3 %scatter_fusion = f32[256,512]{1,0:T(8,128)S(1)} fusion(f32[256,512]{1,0:T(8,128)S(1)} %bitcast.47, s32[256]{0:T(256)S(1)} %bitcast.54, f32[256,512]{1,0:T(8,128)S(1)} %bitcast.50), kind=kCustom, calls=%fused_computation.4 | custom fusion | flops 131072 | bytes 1573888 | tf_op jit(solution)/shard_map/scatter-add | solution.py:64
  43.3 0.4 multiply_reduce_fusion.1
  43.9 0.6 gather_fusion.3
  44.5 4.6 %all-gather = bf16[64,512]{1,0:T(8,128)(2,1)S(1)} all-gather(bf16[32,512]{1,0:T(8,128)(2,1)S(1)} %gather_fusion.3), channel_id=2, replica_groups=mesh['group'=2,'dom'=16] {'group'}, dimensions={0}, use_global_device_ids=true | all-gather | bytes 98304 | tf_op jit(solution)/shard_map/all_gather | solution.py:79
  49.1 2.0 %gather_fusion.2 = bf16[512,512]{1,0:T(8,128)(2,1)S(1)} fusion(bf16[256,512]{1,0:T(8,128)(2,1)S(1)} %multiply_convert_fusion, s32[1024]{0:T(1024)S(1)} %pad_clamp_fusion.1), kind=kCustom, calls=%fused_computation.2 | custom fusion | bytes 1050624 | tf_op jit(solution)/shard_map/gather | solution.py:73
  51.1 0.3 multiply_convert_fusion.1
  51.4 0.8 fusion.4
  52.3 0.3 convolution_multiply_fusion
  52.6 3.7 %scatter_custom_fusion.2 = f32[256,512]{1,0:T(8,128)S(1)} fusion(s32[512]{0:T(512)S(1)} %bitcast.56, f32[512,512]{1,0:T(8,128)S(1)} %convolution_multiply_fusion, f32[]{:T(128)} %constant.15.clone.1), kind=kCustom, calls=%fused_computation.31 | custom fusion | flops 262144 | bytes 524292 | tf_op jit(solution)/shard_map/scatter-add | solution.py:91
  56.4 4.3 %reduce-scatter.3.cloned.1.call-done = bf16[32,512]{1,0:T(8,128)(2,1)} async-done(((bf16[64,512]{1,0:T(8,128)(2,1)}), bf16[32,512]{1,0:T(8,128)(2,1)}) %reduce-scatter.3.cloned.1.call-update) | async-done | bytes 32784 | tf_op jit(solution)/shard_map/reduce_scatter | solution.py:84
  60.6 1.2 scatter_custom_fusion.3
  61.9 0.1 multiply_reduce_fusion
  62.0 2.0 %fusion.5 = f32[1024,512]{1,0:T(8,128)} fusion(bf16[256,512]{1,0:T(8,128)(2,1)S(1)} %divide_convert_fusion, bf16[256,512]{1,0:T(8,128)(2,1)S(1)} %copy-done.2, f32[256,512]{1,0:T(8,128)S(1)} %scatter_custom_fusion.3, f32[256,512]{1,0:T(8,128)S(1)} %get-tuple-element.3, f32[256]{0:T(256)S(1)} %broadcast_multiply_fusion, f32[256]{0:T(256)S(1)} %add_rsqrt_fusion), kind=kOutput, calls=%fused_computation.17 | convolution fusion | flops 270401536 | bytes 3672064 | tf_op jit(solution)/shard_map/dot_general | solution.py:20
  64.0 62.2 %reduce-scatter.5.cloned.1.call-done = f32[64,512]{1,0:T(8,128)} async-done(((f32[1024,512]{1,0:T(8,128)}), f32[64,512]{1,0:T(8,128)}) %reduce-scatter.5.cloned.1.call-update) | async-done | bytes 131088 | tf_op jit(solution)/shard_map/reduce_scatter | solution.py:96
  126.2 0.9 convert_element_type.68
  127.2 4.9 %all-gather.1 = bf16[128,512]{1,0:T(8,128)(2,1)S(1)} all-gather(bf16[64,512]{1,0:T(8,128)(2,1)S(1)} %convert_element_type.68), channel_id=3, replica_groups=mesh['group'=2,'dom'=16] {'group'}, dimensions={0}, use_global_device_ids=true | all-gather | bytes 196608 | tf_op jit(solution)/shard_map/all_gather | solution.py:100
  132.1 0.7 reduce_sum.42
  (31 shorter events, 0.8 us)
Async XLA Ops:
  7.2 36.2 %copy-start = (bf16[512,512]{1,0:T(8,128)(2,1)S(1)}, bf16[512,512]{1,0:T(8,128)(2,1)}, u32[]{:S(2)}) copy-start(bf16[512,512]{1,0:T(8,128)(2,1)} %param.21) | copy-start | bytes 1572868
  7.2 15.1 %copy-start.2 = (bf16[256,512]{1,0:T(8,128)(2,1)S(1)}, bf16[256,512]{1,0:T(8,128)(2,1)}, u32[]{:S(2)}) copy-start(bf16[256,512]{1,0:T(8,128)(2,1)} %param.11) | copy-start | bytes 786436
  8.6 16.1 %all-to-all-start.1 = ((bf16[16,1,16]{2,1,0:T(2,128)(2,1)}), bf16[16,1,16]{2,1,0:T(2,128)(2,1)S(1)}, u32[]{:S(2)}, u32[]{:S(2)}) async-start(bf16[16,1,16]{2,1,0:T(2,128)(2,1)} %compare_convert_fusion), calls=%async_computation.1 | async-start | bytes 16384 | tf_op jit(solution)/shard_map/all_to_all | solution.py:53
  22.3 8.6 %copy-start.3 = (bf16[1,2,4,128,128]{4,3,2,1,0:T(8,128)(2,1)S(1)}, bf16[1,2,4,128,128]{4,3,2,1,0:T(8,128)(2,1)}, u32[]{:S(2)}) copy-start(bf16[1,2,4,128,128]{4,3,2,1,0:T(8,128)(2,1)} %param.13) | copy-start | bytes 786436
  24.8 16.0 %all-to-all-start = ((bf16[16,16,512]{2,1,0:T(8,128)(2,1)}), bf16[16,16,512]{2,1,0:T(8,128)(2,1)S(1)}, u32[]{:S(2)}, u32[]{:S(2)}) async-start(bf16[16,16,512]{2,1,0:T(8,128)(2,1)} %bitcast.10), calls=%async_computation | async-start | bytes 524288 | tf_op jit(solution)/shard_map/all_to_all | solution.py:52
  30.8 29.9 %reduce-scatter.3.cloned.1.call-start = ((), (), s32[]{:S(2)}) async-start(), calls=%async_computation.4 | async-start | bytes 98304 | tf_op jit(solution)/shard_map/reduce_scatter | solution.py:84
  43.9 7.2 %copy-start.1 = (bf16[256,512]{1,0:T(8,128)(2,1)}, bf16[256,512]{1,0:T(8,128)(2,1)S(1)}, u32[]{:S(2)}) copy-start(bf16[256,512]{1,0:T(8,128)(2,1)S(1)} %multiply_convert_fusion) | copy-start | bytes 786436
  49.1 2.0 %copy-start.4 = (s32[1,512]{1,0:T(1,128)S(1)}, s32[1,512]{1,0:T(1,128)}, u32[]{:S(2)}) copy-start(s32[1,512]{1,0:T(1,128)} %param.18) | copy-start | bytes 6148
  52.3 74.0 %reduce-scatter.5.cloned.1.call-start = ((), (), s32[]{:S(2)}) async-start(), calls=%async_computation.5 | async-start | bytes 2228224 | tf_op jit(solution)/shard_map/reduce_scatter | solution.py:96
Sparse Core Ops, SparseCore 0:
  52.4 8.1 reduce-scatter.2
  64.4 61.8 reduce-scatter.4
